TPU v7x, 256 devices: a whole 4x4x8 slice. The times are simulated.
256 devices in a mesh: dp: 16 (over z_hi, y), fsdp: 16 (over x, z_lo, core).
Axes of the slice: x: 4, y: 4, z: 8 (z_hi: 4, z_lo: 2; z = z_hi * 2 + z_lo), core: 2. Of those that a mesh axis runs over, the one named last changes fastest.
Arguments:
- features: bfloat16 [49152, 8192], P(('dp', 'fsdp')), may hold values from -6 to 6
- grad_out: bfloat16 [49152, 8192], P(('dp', 'fsdp')), may hold values from -6 to 6
- weight_tiles: bfloat16 [256, 128, 128], P('fsdp'), may hold values from -0.25 to 0.25
- tile_row: int32 [256], replicated, may hold values from 0 to 63, as said below
- tile_column: int32 [256], replicated, may hold values from 0 to 63, as said below
Outputs:
- grad_features: bfloat16 [49152, 8192], P(('dp', 'fsdp'))
- tile_update: float32 [256, 128, 128], P('fsdp')
Inputs may be any that keep to these rules, and one draw needn't show every extreme that they name: `tile_row`: every tile-row holds exactly 4 stored tiles; the tile-columns of tile-row i are i XOR s for the four values s in (0, 2^a, 2^b, 2^a + 2^b), with two distinct bits a, b drawn per run; the stored order is a random permutation of the pattern. Every tile-column holds exactly 4 stored tiles; no (tile_row, tile_column) pair appears twice.
All inputs are finite; a program needn't handle non-finite values.
Results may differ from a plain program's by a relative error of at most 0.0034.
Values may be sent and summed in bfloat16 or wider, within the bound.
No kernel may reach another device: no remote copies, remote signals or barrier semaphores. Data moves between devices by JAX's collectives and lax.ppermute only.
A program may use at most 128 MiB of HBM per device.

v0:
```python
import math
import jax
import jax.numpy as jnp
from jax import lax
from jax.sharding import PartitionSpec as P


def gelu_slope(value):
    root_term = math.sqrt(2.0 / math.pi)
    inner = root_term * (value + 0.044715 * value * value * value)
    hyper = jnp.tanh(inner)
    return 0.5 * (1.0 + hyper) + 0.5 * value * (1.0 - hyper * hyper) * root_term * (
        1.0 + 3.0 * 0.044715 * value * value
    )


def on_device(features, grad_out, weight_tiles, tile_row, tile_column):
    rows_here = features.shape[0]
    side = weight_tiles.shape[1]
    nblocks = features.shape[1] // side
    total_tiles = tile_row.shape[0]
    per_block = total_tiles // nblocks
    feature_blocks = features.reshape(rows_here, nblocks, side)
    grad_blocks = grad_out.reshape(rows_here, nblocks, side)
    order_rows = jnp.argsort(tile_row, stable=True)
    order_columns = jnp.argsort(tile_column, stable=True)
    columns_by_row = tile_column[order_rows].reshape(nblocks, per_block)
    rows_by_column = tile_row[order_columns].reshape(nblocks, per_block)
    whole = lax.all_gather(weight_tiles, "fsdp", axis=0, tiled=True)
    tiles_by_row = whole[order_rows].reshape(nblocks, per_block, side, side)
    taken = feature_blocks[:, columns_by_row]
    preact = jnp.einsum("rnkc,nkcd->rnd", taken, tiles_by_row, preferred_element_type=jnp.float32)
    slope_grad = (grad_blocks.astype(jnp.float32) * gelu_slope(preact)).astype(jnp.bfloat16)
    tiles_by_column = whole[order_columns].reshape(nblocks, per_block, side, side)
    slopes_taken = slope_grad[:, rows_by_column]
    returned = jnp.einsum(
        "rnkd,nkcd->rnc", slopes_taken, tiles_by_column, preferred_element_type=jnp.float32
    )
    grad_features = (
        (grad_blocks.astype(jnp.float32) + returned)
        .astype(jnp.bfloat16)
        .reshape(rows_here, nblocks * side)
    )
    tile_ids = jnp.arange(
        total_tiles // lax.axis_size("fsdp") * lax.axis_size("fsdp"), dtype=jnp.int32
    )
    columns = tile_column[tile_ids]
    row_ids = tile_row[tile_ids]
    picked = jnp.take(feature_blocks, columns, axis=1)
    slopes = jnp.take(slope_grad, row_ids, axis=1)
    summed = lax.psum_scatter(
        jnp.einsum("rnc,rnd->ncd", picked, slopes, preferred_element_type=jnp.float32),
        "fsdp",
        scatter_dimension=0,
        tiled=True,
    )
    weight_grad = lax.psum(summed, "dp")
    tile_update = weight_grad * lax.rsqrt(
        jnp.mean(weight_grad * weight_grad, axis=(1, 2), keepdims=True) + 1e-06
    )
    return (grad_features, tile_update)


def solution(mesh):
    return jax.shard_map(
        on_device,
        mesh=mesh,
        in_specs=(
            P(("dp", "fsdp"), None),
            P(("dp", "fsdp"), None),
            P("fsdp", None, None),
            P(),
            P(),
        ),
        out_specs=(P(("dp", "fsdp"), None), P("fsdp", None, None)),
        check_vma=False,
    )
```

profile of v0, /device:TPU:8, one launch (start us, length us, event | category | flops | bytes accessed | tf_op | source)
XLA Modules:
  0.0 482.4 jit_solution(4299826176216152528)
XLA Ops:
  7.2 0.7 all-gather.2.cloned.1.call-update
  8.0 4.0 sort.32
  12.0 2.0 gather_fusion.7
  13.9 2.0 gather_fusion.6
  16.0 2.0 gather_fusion.2
  18.2 2.6 copy_bitcast_fusion.1
  20.7 12.8 %gather_fusion.3 = bf16[256,192,128]{2,1,0:T(8,128)(2,1)} fusion(bf16[192,64,128]{2,0,1:T(8,128)(2,1)} %copy_bitcast_fusion.1, s32[1024]{0:T(1024)S(1)} %pad_clamp_fusion.4), kind=kCustom, calls=%fused_computation.5 | custom fusion | bytes 25166848 | tf_op jit(solution)/shard_map/gather | solution.py:31
  33.6 10.8 %gather_fusion.8 = bf16[256,192,128]{2,1,0:T(8,128)(2,1)} fusion(bf16[192,64,128]{2,0,1:T(8,128)(2,1)S(1)} %copy-done.4, s32[1024]{0:T(1024)S(1)} %pad_clamp_fusion.1), kind=kCustom, calls=%fused_computation.clone | custom fusion | bytes 25166848 | tf_op jit(solution)/shard_map/jit(_take)/gather | solution.py:49
  44.4 23.1 %all-gather.2.cloned.1.call-done = bf16[256,128,128]{2,1,0:T(8,128)(2,1)} async-done(((bf16[16,128,128]{2,1,0:T(8,128)(2,1)}), bf16[256,128,128]{2,1,0:T(8,128)(2,1)}) %all-gather.2.cloned.1.call-update) | async-done | bytes 8388624 | tf_op jit(solution)/shard_map/all_gather | solution.py:29
  67.5 12.1 %gather_fusion.1 = bf16[256,128,128]{2,1,0:T(8,128)(2,1)} fusion(bf16[256,128,128]{2,1,0:T(8,128)(2,1)} %all-gather.2.cloned.1.call-done, s32[1024]{0:T(1024)S(1)} %pad_clamp_fusion.5), kind=kCustom, calls=%fused_computation.3 | custom fusion | bytes 16778240 | tf_op jit(solution)/shard_map/gather | solution.py:30
  79.6 11.0 %fusion.13 = bf16[192,64,128]{2,0,1:T(8,128)(2,1)S(1)} fusion(bf16[192,64,4,128]{3,0,2,1:T(8,128)(2,1)} %bitcast.65, bf16[64,4,128,128]{3,2,1,0:T(8,128)(2,1)} %bitcast.68, bf16[192,8192]{1,0:T(8,128)(2,1)} %param.8), kind=kOutput, calls=%fused_computation.25 | convolution fusion | flops 1642070016 | bytes 27262976 | tf_op jit(solution)/shard_map/rnkc,nkcd->rnd/dot_general | solution.py:32
  90.6 10.7 %gather_fusion.9 = bf16[256,192,128]{2,1,0:T(8,128)(2,1)} fusion(bf16[192,64,128]{2,0,1:T(8,128)(2,1)S(1)} %fusion.13, s32[1024]{0:T(1024)S(1)} %pad_clamp_fusion), kind=kCustom, calls=%fused_computation.1.clone | custom fusion | bytes 25166848 | tf_op jit(solution)/shard_map/jit(_take)/gather | solution.py:50
  101.4 14.6 %fusion = f32[256,128,128]{2,1,0:T(8,128)} fusion(bf16[256,192,128]{2,1,0:T(8,128)(2,1)} %gather_fusion.9, bf16[256,192,128]{2,1,0:T(8,128)(2,1)} %gather_fusion.8, pred[256]{0:T(512)(128)(4,1)S(1)} %get-tuple-element.7, pred[256]{0:T(512)(128)(4,1)S(1)} %get-tuple-element.8), kind=kOutput, calls=%fused_computation.10 | convolution fusion | flops 1623195648 | bytes 41943552 | tf_op jit(solution)/shard_map/rnc,rnd->ncd/dot_general | solution.py:52
  116.1 0.6 copy-done.2
  116.7 3.2 sort.31
  119.9 2.2 gather_fusion.4
  122.3 12.4 %gather_fusion.5 = bf16[256,192,128]{2,1,0:T(8,128)(2,1)} fusion(bf16[192,64,128]{2,0,1:T(8,128)(2,1)} %copy-done.5, s32[1024]{0:T(1024)S(1)} %pad_clamp_fusion.3), kind=kCustom, calls=%fused_computation.7 | custom fusion | bytes 25166848 | tf_op jit(solution)/shard_map/gather | solution.py:35
  134.7 12.2 %gather_fusion = bf16[256,128,128]{2,1,0:T(8,128)(2,1)} fusion(bf16[256,128,128]{2,1,0:T(8,128)(2,1)} %all-gather.2.cloned.1.call-done, s32[1024]{0:T(1024)S(1)} %pad_clamp_fusion.6), kind=kCustom, calls=%fused_computation.2 | custom fusion | bytes 16778240 | tf_op jit(solution)/shard_map/gather | solution.py:34
  146.9 155.1 %reduce-scatter.2.cloned.1.call-done = f32[16,128,128]{2,1,0:T(8,128)} async-done(((f32[256,128,128]{2,1,0:T(8,128)}), f32[16,128,128]{2,1,0:T(8,128)}) %reduce-scatter.2.cloned.1.call-update) | async-done | bytes 1048592 | tf_op jit(solution)/shard_map/reduce_scatter | solution.py:51
  302.0 12.5 %fusion.18 = bf16[64,24,8,128]{3,2,1,0:T(8,128)(2,1)} fusion(bf16[64,4,128,128]{3,2,1,0:T(8,128)(2,1)} %bitcast.67, bf16[192,64,4,128]{3,0,2,1:T(8,128)(2,1)} %bitcast.66, bf16[192,8192]{1,0:T(8,128)(2,1)} %param.8), kind=kOutput, calls=%fused_computation.33 | convolution fusion | flops 1615331328 | bytes 27262976 | tf_op jit(solution)/shard_map/rnkd,nkcd->rnc/dot_general | solution.py:36
  314.5 4.4 copy.32
  319.0 153.1 %all-reduce.2.cloned.1.call-done = f32[16,128,128]{2,1,0:T(8,128)} async-done(((f32[16,128,128]{2,1,0:T(8,128)}), f32[16,128,128]{2,1,0:T(8,128)}) %all-reduce.2.cloned.1.call-update) | async-done | bytes 1048592 | tf_op jit(solution)/shard_map/psum | solution.py:57
  472.1 1.4 multiply_reduce_fusion
  473.5 2.3 broadcast_multiply_fusion
  (38 shorter events, 0.7 us)
Async XLA Ops:
  7.2 11.0 %copy-start = (bf16[192,8192]{1,0:T(8,128)(2,1)S(1)}, bf16[192,8192]{1,0:T(8,128)(2,1)}, u32[]{:S(2)}) copy-start(bf16[192,8192]{1,0:T(8,128)(2,1)} %param.7) | copy-start | bytes 9437188
  7.2 60.3 %all-gather.2.cloned.1.call-start = ((), (), s32[]{:S(2)}) async-start(), calls=%async_computation.1 | async-start | bytes 8912896 | tf_op jit(solution)/shard_map/all_gather | solution.py:29
  7.9 294.0 %reduce-scatter.2.cloned.1.call-start = ((), (), s32[]{:S(2)}) async-start(), calls=%async_computation.2 | async-start | bytes 17825792 | tf_op jit(solution)/shard_map/reduce_scatter | solution.py:51
  20.7 12.9 %copy-start.4 = (bf16[192,64,128]{2,0,1:T(8,128)(2,1)S(1)}, bf16[192,64,128]{2,0,1:T(8,128)(2,1)}, u32[]{:S(2)}) copy-start(bf16[192,64,128]{2,0,1:T(8,128)(2,1)} %copy_bitcast_fusion.1) | copy-start | bytes 9437188
  90.6 10.7 %copy-start.5 = (bf16[192,64,128]{2,0,1:T(8,128)(2,1)}, bf16[192,64,128]{2,0,1:T(8,128)(2,1)S(1)}, u32[]{:S(2)}) copy-start(bf16[192,64,128]{2,0,1:T(8,128)(2,1)S(1)} %fusion.13) | copy-start | bytes 9437188
  116.0 0.7 copy-start.2
  116.0 3.9 copy-start.3
  116.0 356.1 %all-reduce.2.cloned.1.call-start = ((), (), s32[]{:S(2)}) async-start(), calls=%async_computation.3 | async-start | bytes 2097152 | tf_op jit(solution)/shard_map/psum | solution.py:57
  302.0 173.9 %copy-start.1 = (bf16[192,8192]{1,0:T(8,128)(2,1)S(1)}, bf16[192,8192]{1,0:T(8,128)(2,1)}, u32[]{:S(2)}) copy-start(bf16[192,8192]{1,0:T(8,128)(2,1)} %param.7) | copy-start | bytes 9437188
Sparse Core Ops, SparseCore 0:
  9.9 57.6 all-gather.1
  116.2 185.7 reduce-scatter.1
  304.6 167.4 all-reduce.1
where the time goes:
time: 483 us; the launch traced here: 482 us
  waiting for transfers between devices  332 us (69%)
  local copies, waits for them, and re-layouts  87.2 us (18%)
  matrix products  38.2 us (8%)
  between operations  13.9 us (3%)
  other arithmetic  11 us (2%)
    reduce_scatter x1, waiting for transfers between devices, on_device(): lax.psum_scatter(jnp.einsum('rnc,rnd->ncd', picked, slopes, preferred_ele...  155 us
    psum x1, waiting for transfers between devices, on_device(): weight_grad = lax.psum(summed, 'dp')  153 us
    all_gather x1, waiting for transfers between devices, on_device(): whole = lax.all_gather(weight_tiles, 'fsdp', axis=0, tiled=True)  23.1 us
    dot_general x1, matrix products, on_device(): jnp.einsum('rnc,rnd->ncd', picked, slopes, preferred_element_type=jnp.flo...  14.6 us
    gather x1, local copies, waits for them, and re-layouts, on_device(): taken = feature_blocks[:, columns_by_row]  12.8 us
    dot_general x1, matrix products, on_device(): jnp.einsum('rnkd,nkcd->rnc', slopes_taken, tiles_by_column, preferred_ele...  12.5 us
    gather x1, local copies, waits for them, and re-layouts, on_device(): slopes_taken = slope_grad[:, rows_by_column]  12.4 us
    gather x1, local copies, waits for them, and re-layouts, on_device(): whole[order_columns].reshape(nblocks, per_block, side, side)  12.2 us
  transfers between devices with their start and end apart: 3, of which 3 were waited for; matrix products, arithmetic and copies ran while one was open for 17% of the time, Pallas kernels for 0%

commit v1 on v0

--- a/solution.py
+++ b/solution.py
@@ -26,7 +26,9 @@
     order_columns = jnp.argsort(tile_column, stable=True)
     columns_by_row = tile_column[order_rows].reshape(nblocks, per_block)
     rows_by_column = tile_row[order_columns].reshape(nblocks, per_block)
-    whole = lax.all_gather(weight_tiles, "fsdp", axis=0, tiled=True)
+    whole = jnp.concatenate(
+        lax.all_to_all(jnp.stack([weight_tiles] * lax.axis_size("fsdp")), "fsdp", 0, 0), axis=0
+    )
     tiles_by_row = whole[order_rows].reshape(nblocks, per_block, side, side)
     taken = feature_blocks[:, columns_by_row]
     preact = jnp.einsum("rnkc,nkcd->rnd", taken, tiles_by_row, preferred_element_type=jnp.float32)

time: 483 us -> 530 us (1.097)
  waiting for transfers between devices: 332 us -> 371 us
  starting transfers between devices: 0.12 us -> 6.02 us
    all_to_all x0 -> x1, waiting for transfers between devices: none -> 60.2 us  [on_device(): lax.all_to_all(jnp.stack([weight_tiles] * lax.axis_size('fsdp')), 'fsdp',...]
    all_gather x1 -> x0, waiting for transfers between devices: 23.1 us -> none  [on_device(): whole = lax.all_gather(weight_tiles, 'fsdp', axis=0, tiled=True)]
    another operation x0 -> x1, local copies, waits for them, and re-layouts: none -> 6.66 us  [on_device(): jnp.stack([weight_tiles] * lax.axis_size('fsdp'))]
    all_to_all x0 -> x1, starting transfers between devices: none -> 5.94 us  [on_device(): lax.all_to_all(jnp.stack([weight_tiles] * lax.axis_size('fsdp')), 'fsdp',...]
  transfers between devices with their start and end apart: 3 -> 3, of which waited for: 3 -> 3; matrix products, arithmetic and copies ran while one was open for 17% -> 15% of each run, Pallas kernels for 0% -> 0%
where the time goes in v1:
time: 530 us
  waiting for transfers between devices  371 us (70%)
  local copies, waits for them, and re-layouts  90.5 us (17%)
  matrix products  38.2 us (7%)
  between operations  14.2 us (3%)
  other arithmetic  10.2 us (2%)
  starting transfers between devices  6.02 us (1%)
    reduce_scatter x1, waiting for transfers between devices, on_device(): lax.psum_scatter(jnp.einsum('rnc,rnd->ncd', picked, slopes, preferred_ele...  157 us
    psum x1, waiting for transfers between devices, on_device(): weight_grad = lax.psum(summed, 'dp')  153 us
    all_to_all x1, waiting for transfers between devices, on_device(): lax.all_to_all(jnp.stack([weight_tiles] * lax.axis_size('fsdp')), 'fsdp',...  60.2 us
    dot_general x1, matrix products, on_device(): jnp.einsum('rnc,rnd->ncd', picked, slopes, preferred_element_type=jnp.flo...  14.7 us
    dot_general x1, matrix products, on_device(): jnp.einsum('rnkd,nkcd->rnc', slopes_taken, tiles_by_column, preferred_ele...  12.5 us
    gather x1, local copies, waits for them, and re-layouts, on_device(): taken = feature_blocks[:, columns_by_row]  12.5 us
    gather x1, local copies, waits for them, and re-layouts, on_device(): whole[order_columns].reshape(nblocks, per_block, side, side)  12.1 us
    gather x1, local copies, waits for them, and re-layouts, on_device(): tiles_by_row = whole[order_rows].reshape(nblocks, per_block, side, side)  12.1 us
  transfers between devices with their start and end apart: 3, of which 3 were waited for; matrix products, arithmetic and copies ran while one was open for 15% of the time, Pallas kernels for 0%

profile of v1, /device:TPU:8, one launch (start us, length us, event | category | flops | bytes accessed | tf_op | source)
XLA Modules:
  0.0 529.9 jit_solution(12233217366795763389)
XLA Ops:
  7.2 6.7 %stack.2 = bf16[16,16,128,128]{3,2,1,0:T(8,128)(2,1)} broadcast(bf16[16,128,128]{2,1,0:T(8,128)(2,1)} %param.9), dimensions={1,2,3} | broadcast | bytes 8912896 | tf_op jit(solution)/shard_map/stack | solution.py:30
  13.8 5.9 %all-to-all-start = ((bf16[16,16,128,128]{3,2,1,0:T(8,128)(2,1)}), bf16[16,16,128,128]{3,2,1,0:T(8,128)(2,1)}, u32[]{:S(2)}, u32[]{:S(2)}) async-start(bf16[16,16,128,128]{3,2,1,0:T(8,128)(2,1)} %stack.2), calls=%async_computation | async-start | bytes 16777216 | tf_op jit(solution)/shard_map/all_to_all | solution.py:30
  19.9 3.2 sort.32
  23.0 1.9 gather_fusion.7
  25.0 1.9 gather_fusion.6
  27.0 1.9 gather_fusion.2
  29.2 2.6 copy_bitcast_fusion.1
  31.7 12.5 %gather_fusion.3 = bf16[256,192,128]{2,1,0:T(8,128)(2,1)} fusion(bf16[192,64,128]{2,0,1:T(8,128)(2,1)} %copy_bitcast_fusion.1, s32[1024]{0:T(1024)S(1)} %pad_clamp_fusion.4), kind=kCustom, calls=%fused_computation.5 | custom fusion | bytes 25166848 | tf_op jit(solution)/shard_map/gather | solution.py:33
  44.3 10.6 %gather_fusion.8 = bf16[256,192,128]{2,1,0:T(8,128)(2,1)} fusion(bf16[192,64,128]{2,0,1:T(8,128)(2,1)S(1)} %copy-done.4, s32[1024]{0:T(1024)S(1)} %pad_clamp_fusion.1), kind=kCustom, calls=%fused_computation.clone | custom fusion | bytes 25166848 | tf_op jit(solution)/shard_map/jit(_take)/gather | solution.py:51
  54.9 60.2 %all-to-all-done = bf16[16,16,128,128]{3,2,1,0:T(8,128)(2,1)} async-done(((bf16[16,16,128,128]{3,2,1,0:T(8,128)(2,1)}), bf16[16,16,128,128]{3,2,1,0:T(8,128)(2,1)}, u32[]{:S(2)}, u32[]{:S(2)}) %all-to-all-start) | async-done | bytes 8388640 | tf_op jit(solution)/shard_map/all_to_all | solution.py:30
  115.1 12.1 %gather_fusion.1 = bf16[256,128,128]{2,1,0:T(8,128)(2,1)} fusion(bf16[256,128,128]{2,1,0:T(8,128)(2,1)} %bitcast, s32[1024]{0:T(1024)S(1)} %pad_clamp_fusion.5), kind=kCustom, calls=%fused_computation.3 | custom fusion | bytes 16778240 | tf_op jit(solution)/shard_map/gather | solution.py:32
  127.2 11.0 %fusion.13 = bf16[192,64,128]{2,0,1:T(8,128)(2,1)S(1)} fusion(bf16[192,64,4,128]{3,0,2,1:T(8,128)(2,1)} %bitcast.66, bf16[64,4,128,128]{3,2,1,0:T(8,128)(2,1)} %bitcast.69, bf16[192,8192]{1,0:T(8,128)(2,1)} %param.8), kind=kOutput, calls=%fused_computation.25 | convolution fusion | flops 1642070016 | bytes 27262976 | tf_op jit(solution)/shard_map/rnkc,nkcd->rnd/dot_general | solution.py:34
  138.2 10.5 %gather_fusion.9 = bf16[256,192,128]{2,1,0:T(8,128)(2,1)} fusion(bf16[192,64,128]{2,0,1:T(8,128)(2,1)S(1)} %fusion.13, s32[1024]{0:T(1024)S(1)} %pad_clamp_fusion), kind=kCustom, calls=%fused_computation.1.clone | custom fusion | bytes 25166848 | tf_op jit(solution)/shard_map/jit(_take)/gather | solution.py:52
  148.7 14.7 %fusion = f32[256,128,128]{2,1,0:T(8,128)} fusion(bf16[256,192,128]{2,1,0:T(8,128)(2,1)} %gather_fusion.9, bf16[256,192,128]{2,1,0:T(8,128)(2,1)} %gather_fusion.8, pred[256]{0:T(512)(128)(4,1)S(1)} %get-tuple-element.7, pred[256]{0:T(512)(128)(4,1)S(1)} %get-tuple-element.8), kind=kOutput, calls=%fused_computation.10 | convolution fusion | flops 1623195648 | bytes 41943552 | tf_op jit(solution)/shard_map/rnc,rnd->ncd/dot_general | solution.py:54
  163.5 3.2 sort.31
  166.7 2.2 gather_fusion.4
  169.1 12.1 %gather_fusion = bf16[256,128,128]{2,1,0:T(8,128)(2,1)} fusion(bf16[256,128,128]{2,1,0:T(8,128)(2,1)} %bitcast, s32[1024]{0:T(1024)S(1)} %pad_clamp_fusion.6), kind=kCustom, calls=%fused_computation.2 | custom fusion | bytes 16778240 | tf_op jit(solution)/shard_map/gather | solution.py:36
  181.2 10.5 %gather_fusion.5 = bf16[256,192,128]{2,1,0:T(8,128)(2,1)} fusion(bf16[192,64,128]{2,0,1:T(8,128)(2,1)S(1)} %fusion.13, s32[1024]{0:T(1024)S(1)} %pad_clamp_fusion.3), kind=kCustom, calls=%fused_computation.7 | custom fusion | bytes 25166848 | tf_op jit(solution)/shard_map/gather | solution.py:37
  191.8 157.3 %reduce-scatter.2.cloned.1.call-done = f32[16,128,128]{2,1,0:T(8,128)} async-done(((f32[256,128,128]{2,1,0:T(8,128)}), f32[16,128,128]{2,1,0:T(8,128)}) %reduce-scatter.2.cloned.1.call-update) | async-done | bytes 1048592 | tf_op jit(solution)/shard_map/reduce_scatter | solution.py:53
  349.1 12.5 %fusion.18 = bf16[64,24,8,128]{3,2,1,0:T(8,128)(2,1)} fusion(bf16[64,4,128,128]{3,2,1,0:T(8,128)(2,1)} %bitcast.68, bf16[192,64,4,128]{3,0,2,1:T(8,128)(2,1)} %bitcast.67, bf16[192,8192]{1,0:T(8,128)(2,1)} %param.8), kind=kOutput, calls=%fused_computation.33 | convolution fusion | flops 1615331328 | bytes 27262976 | tf_op jit(solution)/shard_map/rnkd,nkcd->rnc/dot_general | solution.py:38
  361.6 4.4 copy.27
  366.1 153.2 %all-reduce.2.cloned.1.call-done = f32[16,128,128]{2,1,0:T(8,128)} async-done(((f32[16,128,128]{2,1,0:T(8,128)}), f32[16,128,128]{2,1,0:T(8,128)}) %all-reduce.2.cloned.1.call-update) | async-done | bytes 1048592 | tf_op jit(solution)/shard_map/psum | solution.py:59
  519.2 1.4 multiply_reduce_fusion
  520.7 2.3 broadcast_multiply_fusion
  (36 shorter events, 0.7 us)
Async XLA Ops:
  7.2 22.0 %copy-start = (bf16[192,8192]{1,0:T(8,128)(2,1)S(1)}, bf16[192,8192]{1,0:T(8,128)(2,1)}, u32[]{:S(2)}) copy-start(bf16[192,8192]{1,0:T(8,128)(2,1)} %param.7) | copy-start | bytes 9437188
  13.8 6.0 %copy-start.3 = (s32[256]{0:T(256)S(1)}, s32[256]{0:T(256)}, u32[]{:S(2)}) copy-start(s32[256]{0:T(256)} %param.10) | copy-start | bytes 3076
  13.8 11.1 %copy-start.2 = (s32[256]{0:T(256)S(1)}, s32[256]{0:T(256)}, u32[]{:S(2)}) copy-start(s32[256]{0:T(256)} %param.11) | copy-start | bytes 3076
  13.8 101.3 %all-to-all-start = ((bf16[16,16,128,128]{3,2,1,0:T(8,128)(2,1)}), bf16[16,16,128,128]{3,2,1,0:T(8,128)(2,1)}, u32[]{:S(2)}, u32[]{:S(2)}) async-start(bf16[16,16,128,128]{3,2,1,0:T(8,128)(2,1)} %stack.2), calls=%async_computation | async-start | bytes 16777216 | tf_op jit(solution)/shard_map/all_to_all | solution.py:30
  19.8 329.3 %reduce-scatter.2.cloned.1.call-start = ((), (), s32[]{:S(2)}) async-start(), calls=%async_computation.2 | async-start | bytes 17825792 | tf_op jit(solution)/shard_map/reduce_scatter | solution.py:53
  31.7 12.5 %copy-start.4 = (bf16[192,64,128]{2,0,1:T(8,128)(2,1)S(1)}, bf16[192,64,128]{2,0,1:T(8,128)(2,1)}, u32[]{:S(2)}) copy-start(bf16[192,64,128]{2,0,1:T(8,128)(2,1)} %copy_bitcast_fusion.1) | copy-start | bytes 9437188
  163.4 355.8 %all-reduce.2.cloned.1.call-start = ((), (), s32[]{:S(2)}) async-start(), calls=%async_computation.3 | async-start | bytes 2097152 | tf_op jit(solution)/shard_map/psum | solution.py:59
  349.1 173.9 %copy-start.1 = (bf16[192,8192]{1,0:T(8,128)(2,1)S(1)}, bf16[192,8192]{1,0:T(8,128)(2,1)}, u32[]{:S(2)}) copy-start(bf16[192,8192]{1,0:T(8,128)(2,1)} %param.7) | copy-start | bytes 9437188
Sparse Core Ops, SparseCore 0:
  163.6 185.4 reduce-scatter.1
  351.7 167.5 all-reduce.1
